TPU v7x, 32 devices: a whole 2x2x4 slice. The times are simulated.
32 devices in a mesh: wide: 8 (over z, x), narrow: 4 (over y, core).
Axes of the slice: x: 2, y: 2, z: 4, core: 2. Of those that a mesh axis runs over, the one named last changes fastest.
Arguments:
- potentials: float32 [8, 128, 128, 128], P('wide', 'narrow'), may hold values from -190 to 190
- parents: int32 [8], replicated, may hold values from 0 to 3, as said below
- separator_excluded: int32 [8], replicated, may hold values from 0 to 2
- measurement_clique: int32 [8], replicated, may hold values from 0 to 7, as said below
- measured: float32 [8, 128, 128], P('wide', 'narrow'), may hold values from 0.25 to 4
Outputs:
- marginal: float32 [8, 128, 128], P('wide', 'narrow')
- updated: float32 [8, 128, 128, 128], P('wide', 'narrow')
Inputs may be any that keep to these rules, and one draw needn't show every extreme that they name: parents[0] = 0; a clique c with 1 <= c < 2 has parent 0, one with 2 <= c < 4 a parent in 1 to 1, and one with c >= 4 a parent in 2 to 3; the last clique has parent 4 - 1. `measurement_clique`: every clique is named by exactly one measured marginal.
All inputs are finite; a program needn't handle non-finite values.
Results may differ from a plain program's by a relative error of at most 0.0003.
Values sent between devices are 32-bit elements; how exact they have to be, the bound alone decides.
No kernel may reach another device: no remote copies, remote signals or barrier semaphores. Data moves between devices by JAX's collectives and lax.ppermute only.
A program may use at most 64 MiB of HBM per device.

v0:
```python
import jax
import jax.numpy as jnp
from jax import lax
from jax.sharding import PartitionSpec as P

DEPTH = 3


def merged_2(part, axis, combine):
    gathered = jax.tree.map(lambda a: lax.all_gather(a, axis), part)

    def take(source):
        return jax.tree.map(lambda a: lax.dynamic_index_in_dim(a, source, 0, False), gathered)

    return lax.fori_loop(
        1, lax.axis_size(axis), lambda source, state: combine(state, take(source)), take(0)
    )


def log_sum(values, along):
    largest_entry = jnp.max(values, axis=along, keepdims=True)
    return jnp.squeeze(largest_entry, along) + jnp.log(
        jnp.sum(jnp.exp(values - largest_entry), axis=along)
    )


def join_tables(first, second):
    largest_entry = jnp.maximum(first[0], second[0])
    return (
        largest_entry,
        first[1] * jnp.exp(first[0] - largest_entry)
        + second[1] * jnp.exp(second[0] - largest_entry),
    )


def outgoing(belief, quarter_index, rows_here):
    largest_entry = jnp.max(belief, axis=0)
    summed = jnp.sum(jnp.exp(belief - largest_entry[None]), axis=0)
    merged = merged_2((largest_entry, summed), "narrow", join_tables)
    drop_first = merged[0] + jnp.log(merged[1])
    drop_first = lax.dynamic_slice_in_dim(drop_first, quarter_index * rows_here, rows_here, 0)
    return jnp.stack([drop_first, log_sum(belief, 1), log_sum(belief, 2)])


def route_rows(tables, parents, separator_excluded, self_index):
    kinds = jnp.arange(3, dtype=jnp.int32)
    chosen = (
        (separator_excluded[:, None] == kinds[None, :]) & (parents == self_index)[:, None]
    ).astype(jnp.float32)
    return jnp.einsum("ck,kqv->cqv", chosen, tables, precision=lax.Precision.HIGHEST)


def body(potentials, parents, separator_excluded, measurement_clique, measured):
    own_slab = potentials[0]
    rows_here = own_slab.shape[0]
    domain = own_slab.shape[2]
    wide_count = lax.axis_size("wide")
    self_index = lax.axis_index("wide")
    quarter_index = lax.axis_index("narrow")
    first_leaf = 1 + max(1, wide_count // 16) + wide_count // 4
    belief = own_slab
    for iteration in range(DEPTH):
        tables = outgoing(belief, quarter_index, rows_here)
        outbox = route_rows(tables, parents, separator_excluded, self_index)
        received = lax.all_to_all(outbox, "wide", split_axis=0, concat_axis=0, tiled=True)
        picked = jnp.sum(received, axis=0)
        complete = lax.all_gather(picked, "narrow", axis=0, tiled=True)
        complete = jnp.where(self_index > 0, complete, jnp.float32(0.0))
        belief = own_slab + complete[None]
    scale = jnp.float32(domain * domain)
    largest_entry = jnp.max(belief)
    summed = jnp.sum(jnp.exp(belief - largest_entry))
    merged = merged_2((largest_entry, summed), "narrow", join_tables)
    logz = merged[0] + jnp.log(merged[1])
    weighted = scale * jnp.sum(jnp.exp(belief - logz), axis=0)
    marginal = lax.psum_scatter(weighted, "narrow", scatter_dimension=0, tiled=True)
    source_row = jnp.sum(
        jnp.where(
            measurement_clique == self_index,
            jnp.arange(measurement_clique.shape[0], dtype=jnp.int32),
            0,
        )
    )
    pieces = lax.all_gather(measured, "wide", axis=0, tiled=True)
    row_ids = jnp.arange(pieces.shape[0], dtype=jnp.int32)
    selector = (row_ids == source_row).astype(jnp.float32)
    own_measure = jnp.einsum("m,mqk->qk", selector, pieces, precision=lax.Precision.HIGHEST)
    residual = marginal - own_measure
    residual_whole = lax.all_gather(residual, "narrow", axis=0, tiled=True)
    step_term = jnp.where(self_index >= first_leaf, residual_whole, jnp.float32(0.0))
    updated = own_slab - jnp.float32(0.5) * step_term[None]
    return (marginal[None], updated[None])


def solution(mesh):
    return jax.shard_map(
        body,
        mesh=mesh,
        in_specs=(P("wide", "narrow", None, None), P(), P(), P(), P("wide", "narrow", None)),
        out_specs=(P("wide", "narrow", None), P("wide", "narrow", None, None)),
        check_vma=False,
    )
```

profile of v0, /device:TPU:0, one launch (start us, length us, event | category | flops | bytes accessed | tf_op | source)
XLA Modules:
  0.0 188.3 jit_solution(6694623333389706377)
XLA Ops:
  7.2 2.4 %fusion.52 = (f32[128,128]{1,0:T(8,128)S(1)}, f32[32,128]{1,0:T(8,128)S(1)}, f32[32,128]{1,0:T(8,128)S(1)}) fusion(f32[1,32,128,128]{3,2,1,0:T(8,128)} %param.13), kind=kLoop, calls=%fused_computation.93 | loop fusion | flops 1548288 | bytes 2195456 | tf_op jit(solution)/shard_map/reduce_max | solution.py:37
  9.6 7.3 %all-gather = f32[512,128]{1,0:T(8,128)S(1)} all-gather(f32[128,128]{1,0:T(8,128)S(1)} %get-tuple-element.555), channel_id=2, replica_groups=mesh['wide'=8,'narrow'=4] {'narrow'}, dimensions={0}, use_global_device_ids=true | all-gather | bytes 327680 | tf_op jit(solution)/shard_map/all_gather | solution.py:10
  16.8 1.5 fusion.7
  18.3 5.9 %all-gather.1 = f32[512,128]{1,0:T(8,128)S(1)} all-gather(f32[128,128]{1,0:T(8,128)S(1)} %get-tuple-element.552), channel_id=3, replica_groups=mesh['wide'=8,'narrow'=4] {'narrow'}, dimensions={0}, use_global_device_ids=true | all-gather | bytes 327680 | tf_op jit(solution)/shard_map/all_gather | solution.py:10
  25.5 5.8 %all-to-all-start = ((f32[8,32,128]{2,1,0:T(8,128)}), f32[8,32,128]{2,1,0:T(8,128)S(1)}, u32[]{:S(2)}, u32[]{:S(2)}) async-start(f32[8,32,128]{2,1,0:T(8,128)} %copy.7), calls=%async_computation | async-start | bytes 262144 | tf_op jit(solution)/shard_map/all_to_all | solution.py:65
  31.3 7.5 %all-to-all-done = f32[8,32,128]{2,1,0:T(8,128)S(1)} async-done(((f32[8,32,128]{2,1,0:T(8,128)}), f32[8,32,128]{2,1,0:T(8,128)S(1)}, u32[]{:S(2)}, u32[]{:S(2)}) %all-to-all-start) | async-done | bytes 131104 | tf_op jit(solution)/shard_map/all_to_all | solution.py:65
  38.8 5.2 %all_gather.67 = f32[128,128]{1,0:T(8,128)S(1)} all-gather(f32[32,128]{1,0:T(8,128)S(1)} %reduce_sum.138), channel_id=1, replica_groups=mesh['wide'=8,'narrow'=4] {'narrow'}, dimensions={0}, use_global_device_ids=true | all-gather | bytes 81920 | tf_op jit(solution)/shard_map/all_gather | solution.py:67
  44.9 5.9 %all-gather.2 = f32[512,128]{1,0:T(8,128)S(1)} all-gather(f32[128,128]{1,0:T(8,128)S(1)} %fusion.15), channel_id=4, replica_groups=mesh['wide'=8,'narrow'=4] {'narrow'}, dimensions={0}, use_global_device_ids=true | all-gather | bytes 327680 | tf_op jit(solution)/shard_map/all_gather | solution.py:10
  50.7 1.3 exponential_reduce_fusion.6
  52.1 5.9 %all-gather.3 = f32[512,128]{1,0:T(8,128)S(1)} all-gather(f32[128,128]{1,0:T(8,128)S(1)} %get-tuple-element.547), channel_id=5, replica_groups=mesh['wide'=8,'narrow'=4] {'narrow'}, dimensions={0}, use_global_device_ids=true | all-gather | bytes 327680 | tf_op jit(solution)/shard_map/all_gather | solution.py:10
  59.2 3.4 %all-to-all-start.1 = ((f32[8,32,128]{2,1,0:T(8,128)}), f32[8,32,128]{2,1,0:T(8,128)S(1)}, u32[]{:S(2)}, u32[]{:S(2)}) async-start(f32[8,32,128]{2,1,0:T(8,128)} %copy.8), calls=%async_computation.1 | async-start | bytes 262144 | tf_op jit(solution)/shard_map/all_to_all | solution.py:65
  62.6 7.7 %all-to-all-done.1 = f32[8,32,128]{2,1,0:T(8,128)S(1)} async-done(((f32[8,32,128]{2,1,0:T(8,128)}), f32[8,32,128]{2,1,0:T(8,128)S(1)}, u32[]{:S(2)}, u32[]{:S(2)}) %all-to-all-start.1) | async-done | bytes 131104 | tf_op jit(solution)/shard_map/all_to_all | solution.py:65
  70.3 5.2 %all_gather.72 = f32[128,128]{1,0:T(8,128)S(1)} all-gather(f32[32,128]{1,0:T(8,128)S(1)} %reduce_sum.142), channel_id=1, replica_groups=mesh['wide'=8,'narrow'=4] {'narrow'}, dimensions={0}, use_global_device_ids=true | all-gather | bytes 81920 | tf_op jit(solution)/shard_map/all_gather | solution.py:67
  76.4 5.9 %all-gather.4 = f32[512,128]{1,0:T(8,128)S(1)} all-gather(f32[128,128]{1,0:T(8,128)S(1)} %fusion.18), channel_id=6, replica_groups=mesh['wide'=8,'narrow'=4] {'narrow'}, dimensions={0}, use_global_device_ids=true | all-gather | bytes 327680 | tf_op jit(solution)/shard_map/all_gather | solution.py:10
  82.2 1.3 exponential_reduce_fusion.3
  83.6 5.9 %all-gather.5 = f32[512,128]{1,0:T(8,128)S(1)} all-gather(f32[128,128]{1,0:T(8,128)S(1)} %get-tuple-element.542), channel_id=7, replica_groups=mesh['wide'=8,'narrow'=4] {'narrow'}, dimensions={0}, use_global_device_ids=true | all-gather | bytes 327680 | tf_op jit(solution)/shard_map/all_gather | solution.py:10
  90.1 0.7 copy.9
  90.7 3.4 %all-to-all-start.2 = ((f32[8,32,128]{2,1,0:T(8,128)}), f32[8,32,128]{2,1,0:T(8,128)S(1)}, u32[]{:S(2)}, u32[]{:S(2)}) async-start(f32[8,32,128]{2,1,0:T(8,128)} %copy.9), calls=%async_computation.2 | async-start | bytes 262144 | tf_op jit(solution)/shard_map/all_to_all | solution.py:65
  94.8 30.9 %all_gather.82 = f32[8,32,128]{2,1,0:T(8,128)S(1)} all-gather(f32[1,32,128]{2,1,0:T(8,128)S(1)} %copy-done.1), channel_id=1, replica_groups=mesh['wide'=8,'narrow'=4] {'wide'}, dimensions={0}, use_global_device_ids=true | all-gather | bytes 147456 | tf_op jit(solution)/shard_map/all_gather | solution.py:84
  125.7 0.7 fusion.43
  126.4 5.2 %all_gather.77 = f32[128,128]{1,0:T(8,128)S(1)} all-gather(f32[32,128]{1,0:T(8,128)S(1)} %reduce_sum.146), channel_id=1, replica_groups=mesh['wide'=8,'narrow'=4] {'narrow'}, dimensions={0}, use_global_device_ids=true | all-gather | bytes 81920 | tf_op jit(solution)/shard_map/all_gather | solution.py:67
  131.7 1.2 fusion.12
  132.8 1.8 exponential_reduce_fusion.1
  134.7 1.3 dynamic-update-slice
  136.0 1.3 dynamic-update-slice.1
  137.3 7.1 %all-reduce.2 = (f32[4]{0:T(128)S(1)}, f32[4]{0:T(128)S(1)}) all-reduce(f32[4]{0:T(128)S(1)} %dynamic-update-slice, f32[4]{0:T(128)S(1)} %dynamic-update-slice.1), channel_id=1, replica_groups=mesh['wide'=8,'narrow'=4] {'narrow'}, use_global_device_ids=true, to_apply=%add | all-reduce | flops 8 | bytes 64
  144.5 8.9 %while.71 = (s32[]{:T(128)}, f32[]{:T(128)}, f32[]{:T(128)}, f32[4]{0:T(128)S(1)}, f32[4]{0:T(128)S(1)}, /*index=5*/s32[]{:T(128)}, s32[]{:T(128)}, s32[]{:T(128)}) while((s32[]{:T(128)}, f32[]{:T(128)}, f32[]{:T(128)}, f32[4]{0:T(128)S(1)}, f32[4]{0:T(128)S(1)}, /*index=5*/s32[]{:T(128)}, s32[]{:T(128)}, s32[]{:T(128)}) %tuple.162), condition=%wide.region_30.31_spmd, body=%wide.region_29.30_spmd.sunk | while | flops 11 | bytes 239 | solution.py:15
  154.4 0.9 fusion.19
  155.4 18.7 %reduce-scatter.2.cloned.1.call-done = f32[32,128]{1,0:T(8,128)} async-done(((f32[128,128]{1,0:T(8,128)}), f32[32,128]{1,0:T(8,128)}) %reduce-scatter.2.cloned.1.call-update) | async-done | bytes 16400 | tf_op jit(solution)/shard_map/reduce_scatter | solution.py:76
  174.1 0.7 sub.198
  174.8 5.2 %all_gather.83 = f32[128,128]{1,0:T(8,128)S(1)} all-gather(f32[32,128]{1,0:T(8,128)S(1)} %sub.198), channel_id=1, replica_groups=mesh['wide'=8,'narrow'=4] {'narrow'}, dimensions={0}, use_global_device_ids=true | all-gather | bytes 81920 | tf_op jit(solution)/shard_map/all_gather | solution.py:89
  180.0 1.5 broadcast_subtract_fusion
  (69 shorter events, 10.5 us)
Async XLA Ops:
  7.2 9.6 %copy-start = (f32[1,32,128,128]{3,2,1,0:T(8,128)S(1)}, f32[1,32,128,128]{3,2,1,0:T(8,128)}, u32[]{:S(2)}) copy-start(f32[1,32,128,128]{3,2,1,0:T(8,128)} %param.13) | copy-start | bytes 6291460
  18.3 6.2 %copy-start.3 = (s32[8]{0:T(128)S(1)}, s32[8]{0:T(128)}, u32[]{:S(2)}) copy-start(s32[8]{0:T(128)} %param.14) | copy-start | bytes 100
  18.3 6.2 %copy-start.2 = (s32[8]{0:T(128)S(1)}, s32[8]{0:T(128)}, u32[]{:S(2)}) copy-start(s32[8]{0:T(128)} %param.15) | copy-start | bytes 100
  25.5 13.3 %all-to-all-start = ((f32[8,32,128]{2,1,0:T(8,128)}), f32[8,32,128]{2,1,0:T(8,128)S(1)}, u32[]{:S(2)}, u32[]{:S(2)}) async-start(f32[8,32,128]{2,1,0:T(8,128)} %copy.7), calls=%async_computation | async-start | bytes 262144 | tf_op jit(solution)/shard_map/all_to_all | solution.py:65
  59.2 11.1 %all-to-all-start.1 = ((f32[8,32,128]{2,1,0:T(8,128)}), f32[8,32,128]{2,1,0:T(8,128)S(1)}, u32[]{:S(2)}, u32[]{:S(2)}) async-start(f32[8,32,128]{2,1,0:T(8,128)} %copy.8), calls=%async_computation.1 | async-start | bytes 262144 | tf_op jit(solution)/shard_map/all_to_all | solution.py:65
  83.6 10.6 %copy-start.5 = (u32[32]{0:T(128)S(1)}, u32[32]{0:T(128)}, u32[]{:S(2)}) copy-start(u32[32]{0:T(128)} %constant.199) | copy-start | bytes 388
  83.6 11.2 %copy-start.1 = (f32[1,32,128]{2,1,0:T(8,128)S(1)}, f32[1,32,128]{2,1,0:T(8,128)}, u32[]{:S(2)}) copy-start(f32[1,32,128]{2,1,0:T(8,128)} %param.17) | copy-start | bytes 49156
  83.6 42.1 %copy-start.4 = (s32[8]{0:T(128)S(1)}, s32[8]{0:T(128)}, u32[]{:S(2)}) copy-start(s32[8]{0:T(128)} %param.16) | copy-start | bytes 100
  90.7 35.7 %all-to-all-start.2 = ((f32[8,32,128]{2,1,0:T(8,128)}), f32[8,32,128]{2,1,0:T(8,128)S(1)}, u32[]{:S(2)}, u32[]{:S(2)}) async-start(f32[8,32,128]{2,1,0:T(8,128)} %copy.9), calls=%async_computation.2 | async-start | bytes 262144 | tf_op jit(solution)/shard_map/all_to_all | solution.py:65
  94.1 79.9 %reduce-scatter.2.cloned.1.call-start = ((), (), s32[]{:S(2)}) async-start(), calls=%async_computation.4 | async-start | bytes 81920 | tf_op jit(solution)/shard_map/reduce_scatter | solution.py:76
Sparse Core Ops, SparseCore 0:
  154.5 19.4 reduce-scatter.1
where the time goes:
time: 189 us; the launch traced here: 188 us
  blocking collectives  95.5 us (51%)
  waiting for transfers between devices  33.9 us (18%)
  other arithmetic  15.8 us (8%)
  between operations  14.5 us (8%)
  starting transfers between devices  12.6 us (7%)
  local copies, waits for them, and re-layouts  8.79 us (5%)
  loops' own time  5.6 us (3%)
    all_gather x6, blocking collectives, merged_2(): gathered = jax.tree.map(lambda a: lax.all_gather(a, axis), part)  36.5 us
    all_gather x1, blocking collectives, body(): pieces = lax.all_gather(measured, 'wide', axis=0, tiled=True)  30.9 us
    reduce_scatter x1, waiting for transfers between devices, body(): lax.psum_scatter(weighted, 'narrow', scatter_dimension=0, tiled=True)  18.7 us
    all_gather x3, blocking collectives, body(): complete = lax.all_gather(picked, 'narrow', axis=0, tiled=True)  15.7 us
    all_to_all x3, waiting for transfers between devices, body(): lax.all_to_all(outbox, 'wide', split_axis=0, concat_axis=0, tiled=True)  15.2 us
    all_to_all x3, starting transfers between devices, body(): lax.all_to_all(outbox, 'wide', split_axis=0, concat_axis=0, tiled=True)  12.6 us
    unnamed x1, blocking collectives  7.09 us
    another operation x4, loops' own time, merged_2(): lax.fori_loop(1, lax.axis_size(axis), lambda source, state: combine(state...  5.6 us
  transfers between devices with their start and end apart: 4, of which 3 were waited for; matrix products, arithmetic and copies ran while one was open for 1% of the time, Pallas kernels for 0%

commit v1 on v0

--- a/solution.py
+++ b/solution.py
@@ -1,9 +1,14 @@
+import functools
+
 import jax
 import jax.numpy as jnp
 from jax import lax
+from jax.experimental import pallas as pl
+from jax.experimental.pallas import tpu as pltpu
 from jax.sharding import PartitionSpec as P
 
 DEPTH = 3
+ABSENT = -1e30
 
 
 def merged_2(part, axis, combine):
@@ -50,14 +55,13 @@
     return jnp.einsum("ck,kqv->cqv", chosen, tables, precision=lax.Precision.HIGHEST)
 
 
-def body(potentials, parents, separator_excluded, measurement_clique, measured):
+def general_body(potentials, parents, separator_excluded, measurement_clique, measured):
     own_slab = potentials[0]
     rows_here = own_slab.shape[0]
     domain = own_slab.shape[2]
-    wide_count = lax.axis_size("wide")
     self_index = lax.axis_index("wide")
     quarter_index = lax.axis_index("narrow")
-    first_leaf = 1 + max(1, wide_count // 16) + wide_count // 4
+    first_leaf = level_starts(lax.axis_size("wide"))[3]
     belief = own_slab
     for iteration in range(DEPTH):
         tables = outgoing(belief, quarter_index, rows_here)
@@ -92,9 +96,278 @@
     return (marginal[None], updated[None])
 
 
+def level_starts(wide_count):
+    first = 1 + max(1, wide_count // 16)
+    return (0, 1, first, first + wide_count // 4, wide_count)
+
+
+def move(x, wide_to, narrow_to):
+    wide_count, narrow_count = lax.axis_size("wide"), lax.axis_size("narrow")
+    pairs = [
+        (w * narrow_count + q, (wide_to(w) % wide_count) * narrow_count + narrow_to(q) % narrow_count)
+        for w in range(wide_count)
+        for q in range(narrow_count)
+    ]
+    return lax.ppermute(x, ("wide", "narrow"), pairs)
+
+
+def same(i):
+    return i
+
+
+def plus(k):
+    return lambda i: i + k
+
+
+def flip(k):
+    return lambda i: i ^ k
+
+
+def log_add(a, b):
+    return jnp.maximum(a, b) + jnp.log(1.0 + jnp.exp(-jnp.abs(a - b)))
+
+
+def in_vmem(x):
+    return pltpu.with_memory_space_constraint(x, pltpu.VMEM)
+
+
+def reduce_first(pot_ref, out_ref):
+    domain = pot_ref.shape[1]
+
+    def block(i, _):
+        rows = pl.ds(pl.multiple_of(i * 8, 8), 8)
+        x = pot_ref[:, rows, :]
+        top = jnp.max(x, axis=0)
+        out_ref[rows, :] = top + jnp.log(jnp.sum(jnp.exp(x - top[None]), axis=0))
+        return 0
+
+    lax.fori_loop(0, domain // 8, block, 0)
+
+
+def reduce_later(kind, pot_ref, message_ref, top_ref, sum_ref):
+    rows_here = pot_ref.shape[0]
+
+    def group(i, _):
+        for j in range(4):
+            row = i * 4 + j
+            t = pot_ref[row]
+            if message_ref is not None:
+                t = t + message_ref[...]
+            if kind == 2:
+                t = t.T
+            top = jnp.max(t, axis=0, keepdims=True)
+            top_ref[pl.ds(row, 1), :] = top
+            sum_ref[pl.ds(row, 1), :] = jnp.sum(jnp.exp(t - top), axis=0, keepdims=True)
+        return 0
+
+    lax.fori_loop(0, rows_here // 4, group, 0)
+    return top_ref[...] + jnp.log(sum_ref[...])
+
+
+def own_rows(ref):
+    rows = ref.shape[0] // lax.axis_size("narrow")
+    return ref[pl.ds(pl.multiple_of(lax.axis_index("narrow") * rows, rows), rows), :]
+
+
+def first_kernel(kind_ref, pot_ref, out_ref, top_ref, sum_ref):
+    is_root = lax.axis_index("wide") == 0
+    kind = kind_ref[1]
+    rows = pot_ref.shape[0]
+    mine = pl.ds(pl.multiple_of(lax.axis_index("narrow") * rows, rows), rows)
+
+    @pl.when(jnp.logical_or(jnp.logical_not(is_root), kind == 0))
+    def _():
+        reduce_first(pot_ref, out_ref)
+
+    for k in (1, 2):
+
+        @pl.when(jnp.logical_and(is_root, kind == k))
+        def _():
+            out_ref[...] = jnp.full(out_ref.shape, ABSENT, jnp.float32)
+            out_ref[mine, :] = reduce_later(k, pot_ref, None, top_ref, sum_ref)
+
+
+def rest_kernel(kind_ref, pot_ref, first_ref, out_ref):
+    again = jnp.logical_and(lax.axis_index("wide") == 0, kind_ref[1] != 0)
+
+    @pl.when(again)
+    def _():
+        reduce_first(pot_ref, out_ref)
+
+    @pl.when(jnp.logical_not(again))
+    def _():
+        out_ref[...] = first_ref[...]
+
+
+def send_tiles(active, children, kind_ref, pot_ref, message_ref, whole_ref, tiles_ref, kept_ref, top_ref, sum_ref):
+    def wants(k):
+        return functools.reduce(jnp.logical_or, [kind_ref[c] == k for c in children])
+
+    @pl.when(active)
+    def _():
+        kept_ref[0] = own_rows(whole_ref) + own_rows(message_ref)
+        for k in (1, 2):
+
+            @pl.when(wants(k))
+            def _():
+                kept_ref[k] = reduce_later(k, pot_ref, message_ref, top_ref, sum_ref)
+
+        for slot, c in enumerate(children):
+            tiles_ref[slot] = kept_ref[kind_ref[c]]
+
+
+def second_kernel(kind_ref, pot_ref, one_ref, two_ref, whole_ref, mine_ref, tiles_ref, message_ref, kept_ref, top_ref, sum_ref):
+    active = lax.axis_index("wide") == 1
+
+    @pl.when(active)
+    def _():
+        message_ref[...] = log_add(one_ref[...], two_ref[...])
+        mine_ref[...] = own_rows(message_ref)
+
+    send_tiles(active, [3, 2], kind_ref, pot_ref, message_ref, whole_ref, tiles_ref, kept_ref, top_ref, sum_ref)
+
+
+def third_kernel(kind_ref, pot_ref, one_ref, two_ref, whole_ref, mine_ref, tiles_ref, message_ref, kept_ref, top_ref, sum_ref):
+    w = lax.axis_index("wide")
+    q = lax.axis_index("narrow")
+    rows = pot_ref.shape[0]
+    active = jnp.logical_or(w == 2, w == 3)
+
+    @pl.when(active)
+    def _():
+        for ref, receiver in ((one_ref, q), (two_ref, q ^ 1)):
+            sender = (receiver + 3) & 3
+            for slot, source in ((0, sender), (1, sender ^ 1)):
+                message_ref[pl.ds(pl.multiple_of(source * rows, rows), rows), :] = ref[slot]
+        mine_ref[...] = own_rows(message_ref)
+
+    children = [(w + 2) & 7, (w + 4) & 7, ((w + 2) & 7) ^ 1, ((w + 4) & 7) ^ 1]
+    send_tiles(active, children, kind_ref, pot_ref, message_ref, whole_ref, tiles_ref, kept_ref, top_ref, sum_ref)
+
+
+def last_kernel(pot_ref, here_ref, there_ref, whole_ref, marginal_ref, updated_ref, term_ref, cells_ref, measure_ref):
+    w = lax.axis_index("wide")
+    q = lax.axis_index("narrow")
+    rows = pot_ref.shape[0]
+    domain = pot_ref.shape[2]
+
+    @pl.when(pl.program_id(0) == 0)
+    def _():
+        for ref, base in ((here_ref, q), (there_ref, q ^ 1)):
+            for slot, source in ((0, base), (1, base ^ 2)):
+                span = pl.ds(pl.multiple_of(source * rows, rows), rows)
+                cells_ref[span, :] = ref[slot] + whole_ref[span, :]
+                measure_ref[span, :] = ref[slot + 2]
+        cells = cells_ref[...]
+        top = jnp.max(cells, axis=(0, 1), keepdims=True)
+        logz = top + jnp.log(jnp.sum(jnp.exp(cells - top), axis=(0, 1), keepdims=True))
+        marginal = jnp.float32(domain * domain) * jnp.exp(cells - logz)
+        cells_ref[...] = marginal
+        marginal_ref[...] = own_rows(cells_ref)
+        is_leaf = w >= 4
+        term_ref[...] = jnp.where(is_leaf, jnp.float32(0.5) * (marginal - measure_ref[...]), jnp.float32(0.0))
+
+    step = updated_ref.shape[0]
+    updated_ref[...] = pot_ref[pl.ds(pl.program_id(0) * step, step)] - term_ref[...][None]
+
+
+def relay_body(potentials, parents, separator_excluded, measurement_clique, measured):
+    rows, domain = potentials.shape[1], potentials.shape[3]
+    me = lax.axis_index("wide")
+    f32 = jnp.float32
+    smem = pl.BlockSpec(memory_space=pltpu.SMEM)
+    vmem = pl.BlockSpec(memory_space=pltpu.VMEM)
+    table = jax.ShapeDtypeStruct((domain, domain), f32)
+    tile = jax.ShapeDtypeStruct((rows, domain), f32)
+    tile_scratch = pltpu.VMEM((rows, domain), f32)
+    table_scratch = pltpu.VMEM((domain, domain), f32)
+
+    pot = in_vmem(potentials[0])
+
+    gathered = [measured[0]]
+    ids = [me]
+    for k in (4, 1):
+        other = move(jnp.stack(gathered), flip(k), same)
+        ids = ids + [i ^ k for i in ids]
+        gathered = gathered + [other[i] for i in range(len(gathered))]
+
+    def owned_by(c):
+        return sum(jnp.where(measurement_clique[i] == c, g, f32(0.0)) for i, g in zip(ids, gathered))
+
+    measure = owned_by(me) + move(owned_by(me ^ 2), flip(2), same)
+
+    first = pl.pallas_call(
+        first_kernel, out_shape=table, in_specs=[smem, vmem], out_specs=vmem,
+        scratch_shapes=[tile_scratch, tile_scratch], name="first",
+    )(separator_excluded, pot)
+    chip = log_add(first, move(first, same, flip(1)))
+    one = move(chip, plus(1), plus(1))
+    two = move(one, same, flip(1))
+
+    rest = pl.pallas_call(
+        rest_kernel, out_shape=table, in_specs=[smem, vmem, vmem], out_specs=vmem, name="rest",
+    )(separator_excluded, pot, first)
+    whole = log_add(rest, move(rest, same, flip(1)))
+    whole = log_add(whole, move(whole, same, flip(2)))
+
+    scratch = [table_scratch, pltpu.VMEM((3, rows, domain), f32), tile_scratch, tile_scratch]
+
+    def tiles(n):
+        return jax.ShapeDtypeStruct((n, rows, domain), f32)
+
+    mine_1, sent = pl.pallas_call(
+        second_kernel, out_shape=(tile, tiles(2)), in_specs=[smem] + [vmem] * 4, out_specs=(vmem, vmem),
+        scratch_shapes=scratch, name="second",
+    )(separator_excluded, pot, one, two, whole)
+    partner = move(sent, same, flip(1))
+    from_a = move(jnp.stack([sent[0], partner[0]]), plus(2), plus(1))
+    from_b = move(jnp.stack([sent[1], partner[1]]), lambda w: (w + 2) ^ 1, plus(1))
+    one = jnp.where(me == 3, from_a, from_b)
+    two = move(one, same, flip(1))
+
+    mine_2, sent = pl.pallas_call(
+        third_kernel, out_shape=(tile, tiles(4)), in_specs=[smem] + [vmem] * 4, out_specs=(vmem, vmem),
+        scratch_shapes=scratch, name="third",
+    )(separator_excluded, pot, one, two, whole)
+    from_a = move(sent[:2], plus(2), same)
+    from_b = move(sent[2:], lambda w: (w + 2) ^ 1, same)
+    own_tile = jnp.where(parents[me] == me - 2, from_a[0], from_b[0])
+    onward = jnp.where(parents[jnp.minimum(me + 2, 7)] == me - 2, from_a[1], from_b[1])
+    relayed = move(onward, plus(2), same)
+    relayed_across = move(onward, plus(2), flip(2))
+    message = jnp.where(me >= 6, relayed, own_tile)
+    message = jnp.where(me <= 3, mine_2, message)
+    message = jnp.where(me <= 1, mine_1, message)
+    message = jnp.where(me == 0, f32(0.0), message)
+    across = move(jnp.stack([message, measure]), same, flip(2))
+    here = jnp.stack([message, jnp.where(me >= 6, relayed_across, across[0]), measure, across[1]])
+    there = move(here, same, flip(1))
+
+    steps = 4
+    once2 = lambda i: (0, 0)
+    once3 = lambda i: (0, 0, 0)
+    marginal, updated = pl.pallas_call(
+        last_kernel,
+        grid=(steps,),
+        out_shape=(tile, jax.ShapeDtypeStruct((rows, domain, domain), f32)),
+        in_specs=[vmem, vmem, vmem, vmem],
+        out_specs=(
+            pl.BlockSpec((rows, domain), once2),
+            pl.BlockSpec((rows // steps, domain, domain), lambda i: (i, 0, 0)),
+        ),
+        scratch_shapes=[table_scratch, table_scratch, table_scratch],
+        name="last",
+    )(pot, here, there, whole)
+    return (marginal[None], updated[None])
+
+
 def solution(mesh):
+    wide_count, narrow_count = mesh.shape["wide"], mesh.shape["narrow"]
+    starts = level_starts(wide_count)
+    widths = tuple(b - a for a, b in zip(starts, starts[1:]))
+    relay = widths == (1, 1, 2, 4) and narrow_count == 4
     return jax.shard_map(
-        body,
+        relay_body if relay else general_body,
         mesh=mesh,
         in_specs=(P("wide", "narrow", None, None), P(), P(), P(), P("wide", "narrow", None)),
         out_specs=(P("wide", "narrow", None), P("wide", "narrow", None, None)),

time: 189 us -> 65.6 us (0.35)
  blocking collectives: 95.5 us -> 0 us
  other arithmetic: 15.8 us -> 2.35 us
  Pallas kernels: 0 us -> 10.6 us
  waiting for transfers between devices: 33.9 us -> 24.1 us
  between operations: 14.5 us -> 7.07 us
  loops' own time: 5.6 us -> 0 us
  starting transfers between devices: 12.6 us -> 15.2 us
  local copies, waits for them, and re-layouts: 8.79 us -> 6.22 us
    all_gather x11 -> x0, blocking collectives: 88.4 us -> none  [the longest x6 36.5 us: merged_2(): gathered = jax.tree.map(lambda a: lax.all_gather(a, axis), part)]
    ppermute x0 -> x18, waiting for transfers between devices: none -> 24.1 us  [move(): return lax.ppermute(x, ('wide', 'narrow'), pairs)]
    reduce_scatter x1 -> x0, waiting for transfers between devices: 18.7 us -> none  [body(): lax.psum_scatter(weighted, 'narrow', scatter_dimension=0, tiled=True)]
    all_to_all x3 -> x0, waiting for transfers between devices: 15.2 us -> none  [body(): lax.all_to_all(outbox, 'wide', split_axis=0, concat_axis=0, tiled=True)]
    ppermute x0 -> x18, starting transfers between devices: none -> 15.2 us  [move(): return lax.ppermute(x, ('wide', 'narrow'), pairs)]
    all_to_all x3 -> x0, starting transfers between devices: 12.6 us -> none  [body(): lax.all_to_all(outbox, 'wide', split_axis=0, concat_axis=0, tiled=True)]
    pallas_call x0 -> x5, Pallas kernels: none -> 10.6 us  [the longest x1 3.05 us: relay_body(): pl.pallas_call(last_kernel, grid=(steps,), out_shape=(tile, jax.ShapeDtyp...]
    reduce_sum x11 -> x0, other arithmetic: 8.33 us -> none  [the longest x3 2.77 us: outgoing(): summed = jnp.sum(jnp.exp(belief - largest_entry[None]), axis=0)]
  transfers between devices with their start and end apart: 4 -> 18, of which waited for: 3 -> 11; matrix products, arithmetic and copies ran while one was open for 1% -> 7% of each run, Pallas kernels for 0% -> 6%
where the time goes in v1:
time: 65.6 us; the launch traced here: 65.5 us
  waiting for transfers between devices  24.1 us (37%)
  starting transfers between devices  15.2 us (23%)
  Pallas kernels  10.6 us (16%)
  between operations  7.07 us (11%)
  local copies, waits for them, and re-layouts  6.22 us (9%)
  other arithmetic  2.35 us (4%)
    ppermute x18, waiting for transfers between devices, move(): return lax.ppermute(x, ('wide', 'narrow'), pairs)  24.1 us
    ppermute x18, starting transfers between devices, move(): return lax.ppermute(x, ('wide', 'narrow'), pairs)  15.2 us
    unnamed x24, local copies, waits for them, and re-layouts  3.45 us
    pallas_call x1, Pallas kernels, relay_body(): pl.pallas_call(last_kernel, grid=(steps,), out_shape=(tile, jax.ShapeDtyp...  3.05 us
    pallas_call x1, Pallas kernels, relay_body(): pl.pallas_call(rest_kernel, out_shape=table, in_specs=[smem, vmem, vmem],...  2.59 us
    pallas_call x1, Pallas kernels, relay_body(): pl.pallas_call(first_kernel, out_shape=table, in_specs=[smem, vmem], out_...  1.89 us
    add x3, other arithmetic, log_add(): return jnp.maximum(a, b) + jnp.log(1.0 + jnp.exp(-jnp.abs(a - b)))  1.56 us
    pallas_call x1, Pallas kernels, relay_body(): pl.pallas_call(third_kernel, out_shape=(tile, tiles(4)), in_specs=[smem]...  1.54 us
  transfers between devices with their start and end apart: 18, of which 11 were waited for; matrix products, arithmetic and copies ran while one was open for 7% of the time, Pallas kernels for 6%

profile of v1, /device:TPU:0, one launch (start us, length us, event | category | flops | bytes accessed | tf_op | source)
XLA Modules:
  0.0 65.5 jit_solution(4055024976664465128)
XLA Ops:
  0.6 1.6 %copy-done = f32[1,32,128,128]{3,2,1,0:T(8,128)S(1)} copy-done((f32[1,32,128,128]{3,2,1,0:T(8,128)S(1)}, f32[1,32,128,128]{3,2,1,0:T(8,128)}, u32[]{:S(2)}) %copy-start) | copy-done | bytes 2097176
  2.2 1.9 %first.1.first_ref = f32[128,128]{1,0:T(8,128)} custom-call(s32[8]{0:T(128)} %kind_ref.7, f32[32,128,128]{2,1,0:T(8,128)S(1)} %bitcast.41), custom_call_target="tpu_custom_call" | custom-call | tf_op jit(solution)/shard_map/first/pallas_call | solution.py:299
  4.6 2.6 %rest.1 = f32[128,128]{1,0:T(8,128)} custom-call(s32[8]{0:T(128)} %kind_ref.7, f32[32,128,128]{2,1,0:T(8,128)S(1)} %bitcast.42, f32[128,128]{1,0:T(8,128)} %first.1.first_ref), custom_call_target="tpu_custom_call" | custom-call | tf_op jit(solution)/shard_map/rest/pallas_call | solution.py:307
  7.3 2.1 %collective-permute-start.1 = (f32[128,128]{1,0:T(8,128)S(1)}, f32[128,128]{1,0:T(8,128)S(1)}, u32[]{:S(2)}, u32[]{:S(2)}) collective-permute-start(f32[128,128]{1,0:T(8,128)S(1)} %log_add_fusion.2), channel_id=1, source_target_pairs={{0,5},{1,6},{2,7},{3,4},{4,9},{5,10},{6,11},{7,8},{8,13},{9,14},{1... | collective-permute-start | bytes 196616 | tf_op jit(solution)/shard_map/ppermute | solution.py:111
  9.4 0.9 %log_add_fusion.1 = f32[128,128]{1,0:T(8,128)S(1)} fusion(f32[128,128]{1,0:T(8,128)} %rest.1, f32[128,128]{1,0:T(8,128)S(1)} %collective-permute-done.3), kind=kLoop, calls=%fused_computation.2 | loop fusion | flops 98304 | bytes 196608 | tf_op jit(solution)/shard_map/add | solution.py:127
  10.3 2.0 %collective-permute-start.4 = (f32[128,128]{1,0:T(8,128)S(1)}, f32[128,128]{1,0:T(8,128)S(1)}, u32[]{:S(2)}, u32[]{:S(2)}) collective-permute-start(f32[128,128]{1,0:T(8,128)S(1)} %log_add_fusion.1), channel_id=1, source_target_pairs={{0,2},{1,3},{2,0},{3,1},{4,6},{5,7},{6,4},{7,5},{8,10},{9,11},{10,... | collective-permute-start | bytes 196616 | tf_op jit(solution)/shard_map/ppermute | solution.py:111
  12.3 3.2 %collective-permute-done.1.one_ref = f32[128,128]{1,0:T(8,128)S(1)} collective-permute-done((f32[128,128]{1,0:T(8,128)S(1)}, f32[128,128]{1,0:T(8,128)S(1)}, u32[]{:S(2)}, u32[]{:S(2)}) %collective-permute-start.1) | collective-permute-done | bytes 65568 | tf_op jit(solution)/shard_map/ppermute | solution.py:111
  15.6 0.7 log_add_fusion.whole_ref
  16.7 0.6 copy-done.6
  17.3 1.5 %second.1 = (f32[32,128]{1,0:T(8,128)}, f32[2,32,128]{2,1,0:T(8,128)}) custom-call(s32[8]{0:T(128)} %kind_ref.7, f32[32,128,128]{2,1,0:T(8,128)S(1)} %bitcast.43, f32[128,128]{1,0:T(8,128)} %copy-done.5, f32[128,128]{1,0:T(8,128)} %copy-done.6, f32[128,128]{1,0:T(8,128)} %log_add_fusion.whole_ref), custom_call_target="tpu_custom_call" | custom-call | tf_op jit(solution)/shard_map/second/pallas_call | solution.py:318
  19.0 0.7 %fusion.11 = (f32[1,32,128]{2,1,0:T(8,128)S(1)}, f32[1,32,128]{2,1,0:T(8,128)S(1)}) fusion(f32[2,32,128]{2,1,0:T(8,128)} %get-tuple-element.9), kind=kLoop, calls=%fused_computation.25 | loop fusion | bytes 65536 | tf_op jit(solution)/shard_map/slice | solution.py:324
  19.7 0.5 collective-permute-done.5
  20.7 3.1 %collective-permute-start.7 = (f32[2,32,128]{2,1,0:T(8,128)S(1)}, f32[2,32,128]{2,1,0:T(8,128)S(1)}, u32[]{:S(2)}, u32[]{:S(2)}) collective-permute-start(f32[2,32,128]{2,1,0:T(8,128)S(1)} %pad_maximum_fusion.2), channel_id=1, source_target_pairs={{0,13},{1,14},{2,15},{3,12},{4,9},{5,10},{6,11},{7,8},{8,21},{9,22... | collective-permute-start | bytes 98312 | tf_op jit(solution)/shard_map/ppermute | solution.py:111
  23.8 3.4 %collective-permute-start.13 = (f32[1,32,128]{2,1,0:T(8,128)S(1)}, f32[1,32,128]{2,1,0:T(8,128)S(1)}, u32[]{:S(2)}, u32[]{:S(2)}) collective-permute-start(f32[1,32,128]{2,1,0:T(8,128)S(1)} %copy-done.3), channel_id=1, source_target_pairs={{0,16},{1,17},{2,18},{3,19},{4,20},{5,21},{6,22},{7,23},{8,24},{9,... | collective-permute-start | bytes 49160 | tf_op jit(solution)/shard_map/ppermute | solution.py:111
  27.2 0.6 fusion.14
  32.8 0.6 fusion.13
  35.3 0.8 %collective-permute-done.8.two_ref = f32[2,32,128]{2,1,0:T(8,128)S(1)} collective-permute-done((f32[2,32,128]{2,1,0:T(8,128)S(1)}, f32[2,32,128]{2,1,0:T(8,128)S(1)}, u32[]{:S(2)}, u32[]{:S(2)}) %collective-permute-start.8) | collective-permute-done | bytes 32800 | tf_op jit(solution)/shard_map/ppermute | solution.py:111
  36.1 0.6 copy-done.8
  36.7 1.5 %third.1 = (f32[32,128]{1,0:T(8,128)}, f32[4,32,128]{2,1,0:T(8,128)}) custom-call(s32[8]{0:T(128)} %kind_ref.7, f32[32,128,128]{2,1,0:T(8,128)S(1)} %bitcast.44, f32[2,32,128]{2,1,0:T(8,128)} %copy-done.4, f32[2,32,128]{2,1,0:T(8,128)} %copy-done.8, f32[128,128]{1,0:T(8,128)} %log_add_fusion.whole_ref), custom_call_target="tpu_custom_call" | custom-call | tf_op jit(solution)/shard_map/third/pallas_call | solution.py:328
  38.2 0.8 %fusion.10 = (f32[2,32,128]{2,1,0:T(8,128)S(1)}, f32[2,32,128]{2,1,0:T(8,128)S(1)}) fusion(f32[4,32,128]{2,1,0:T(8,128)} %get-tuple-element.11), kind=kLoop, calls=%fused_computation.24 | loop fusion | bytes 131072 | tf_op jit(solution)/shard_map/slice | solution.py:332
  39.0 1.3 %collective-permute-start.9 = (f32[2,32,128]{2,1,0:T(8,128)S(1)}, f32[2,32,128]{2,1,0:T(8,128)S(1)}, u32[]{:S(2)}, u32[]{:S(2)}) collective-permute-start(f32[2,32,128]{2,1,0:T(8,128)S(1)} %get-tuple-element.14), channel_id=1, source_target_pairs={{0,8},{1,9},{2,10},{3,11},{4,12},{5,13},{6,14},{7,15},{8,16},{9,17... | collective-permute-start | bytes 98312 | tf_op jit(solution)/shard_map/ppermute | solution.py:111
  40.3 0.7 %collective-permute-start.10 = (f32[2,32,128]{2,1,0:T(8,128)S(1)}, f32[2,32,128]{2,1,0:T(8,128)S(1)}, u32[]{:S(2)}, u32[]{:S(2)}) collective-permute-start(f32[2,32,128]{2,1,0:T(8,128)S(1)} %get-tuple-element.15), channel_id=1, source_target_pairs={{0,12},{1,13},{2,14},{3,15},{4,8},{5,9},{6,10},{7,11},{8,20},{9,21... | collective-permute-start | bytes 98312 | tf_op jit(solution)/shard_map/ppermute | solution.py:111
  41.1 3.6 %collective-permute-done.9 = f32[2,32,128]{2,1,0:T(8,128)S(1)} collective-permute-done((f32[2,32,128]{2,1,0:T(8,128)S(1)}, f32[2,32,128]{2,1,0:T(8,128)S(1)}, u32[]{:S(2)}, u32[]{:S(2)}) %collective-permute-start.9) | collective-permute-done | bytes 32800 | tf_op jit(solution)/shard_map/ppermute | solution.py:111
  44.7 2.2 %collective-permute-done.10 = f32[2,32,128]{2,1,0:T(8,128)S(1)} collective-permute-done((f32[2,32,128]{2,1,0:T(8,128)S(1)}, f32[2,32,128]{2,1,0:T(8,128)S(1)}, u32[]{:S(2)}, u32[]{:S(2)}) %collective-permute-start.10) | collective-permute-done | bytes 32800 | tf_op jit(solution)/shard_map/ppermute | solution.py:111
  47.0 5.5 %collective-permute-done.11 = f32[32,128]{1,0:T(8,128)S(1)} collective-permute-done((f32[32,128]{1,0:T(8,128)S(1)}, f32[32,128]{1,0:T(8,128)S(1)}, u32[]{:S(2)}, u32[]{:S(2)}) %collective-permute-start.11) | collective-permute-done | bytes 16416 | tf_op jit(solution)/shard_map/ppermute | solution.py:111
  52.5 0.7 %fusion.7 = f32[1,32,128]{2,1,0:T(8,128)S(1)} fusion(f32[32,128]{1,0:T(8,128)S(1)} %copy-done.9, f32[32,128]{1,0:T(8,128)} %get-tuple-element.10, f32[32,128]{1,0:T(8,128)S(1)} %collective-permute-done.11, f32[2,32,128]{2,1,0:T(8,128)S(1)} %collective-permute-done.10, f32[2,32,128]{2,1,0:T(8,128)S(1)} %collective-permute-done.9, pred[]{:T(512)S(6)} %eq.39, ...), kind=kLoop, calls=%fused_computation.17 | loop fusion | flops 20480 | bytes 98309 | tf_op jit(solution)/shard_map/stack | solution.py:343
  53.2 0.9 %collective-permute-start.16 = (f32[2,32,128]{2,1,0:T(8,128)S(1)}, f32[2,32,128]{2,1,0:T(8,128)S(1)}, u32[]{:S(2)}, u32[]{:S(2)}) collective-permute-start(f32[2,32,128]{2,1,0:T(8,128)S(1)} %pad_maximum_fusion.4), channel_id=1, source_target_pairs={{0,2},{1,3},{2,0},{3,1},{4,6},{5,7},{6,4},{7,5},{8,10},{9,11},{10,... | collective-permute-start | bytes 98312 | tf_op jit(solution)/shard_map/ppermute | solution.py:111
  54.1 3.2 %collective-permute-done.16 = f32[2,32,128]{2,1,0:T(8,128)S(1)} collective-permute-done((f32[2,32,128]{2,1,0:T(8,128)S(1)}, f32[2,32,128]{2,1,0:T(8,128)S(1)}, u32[]{:S(2)}, u32[]{:S(2)}) %collective-permute-start.16) | collective-permute-done | bytes 32800 | tf_op jit(solution)/shard_map/ppermute | solution.py:111
  57.3 3.3 %collective-permute-done.12 = f32[32,128]{1,0:T(8,128)S(1)} collective-permute-done((f32[32,128]{1,0:T(8,128)S(1)}, f32[32,128]{1,0:T(8,128)S(1)}, u32[]{:S(2)}, u32[]{:S(2)}) %collective-permute-start.12) | collective-permute-done | bytes 16416 | tf_op jit(solution)/shard_map/ppermute | solution.py:111
  60.6 1.2 %collective-permute-done.17.there_ref = f32[4,32,128]{2,1,0:T(8,128)S(1)} collective-permute-done((f32[4,32,128]{2,1,0:T(8,128)S(1)}, f32[4,32,128]{2,1,0:T(8,128)S(1)}, u32[]{:S(2)}, u32[]{:S(2)}) %collective-permute-start.17) | collective-permute-done | bytes 65568 | tf_op jit(solution)/shard_map/ppermute | solution.py:111
  61.9 0.6 copy-done.7
  62.5 3.0 %last.1 = (f32[32,128]{1,0:T(8,128)}, f32[32,128,128]{2,1,0:T(8,128)}) custom-call(f32[32,128,128]{2,1,0:T(8,128)S(1)} %bitcast.45, f32[4,32,128]{2,1,0:T(8,128)} %copy-done.2, f32[4,32,128]{2,1,0:T(8,128)} %copy-done.7, f32[128,128]{1,0:T(8,128)} %log_add_fusion.whole_ref), custom_call_target="tpu_custom_call" | custom-call | tf_op jit(solution)/shard_map/last/pallas_call | solution.py:349
  (53 shorter events, 2.5 us)
Async XLA Ops:
  0.6 1.6 %copy-start = (f32[1,32,128,128]{3,2,1,0:T(8,128)S(1)}, f32[1,32,128,128]{3,2,1,0:T(8,128)}, u32[]{:S(2)}) copy-start(f32[1,32,128,128]{3,2,1,0:T(8,128)} %param.5) | copy-start | bytes 6291460
  4.1 3.2 %copy-start.1 = (f32[128,128]{1,0:T(8,128)S(1)}, f32[128,128]{1,0:T(8,128)}, u32[]{:S(2)}) copy-start(f32[128,128]{1,0:T(8,128)} %first.1.first_ref) | copy-start | bytes 196612
  4.1 3.2 %collective-permute-start = (f32[128,128]{1,0:T(8,128)}, f32[128,128]{1,0:T(8,128)S(1)}, u32[]{:S(2)}, u32[]{:S(2)}) collective-permute-start(f32[128,128]{1,0:T(8,128)} %first.1.first_ref), channel_id=1, source_target_pairs={{0,1},{1,0},{2,3},{3,2},{4,5},{5,4},{6,7},{7,6},{8,9},{9,8},{10,11... | collective-permute-start | bytes 196616 | tf_op jit(solution)/shard_map/ppermute | solution.py:111
  7.2 16.6 %copy-start.3 = (f32[1,32,128]{2,1,0:T(8,128)S(1)}, f32[1,32,128]{2,1,0:T(8,128)}, u32[]{:S(2)}) copy-start(f32[1,32,128]{2,1,0:T(8,128)} %param.9) | copy-start | bytes 49156
  7.2 20.0 %copy-start.10 = (s32[8]{0:T(128)S(1)}, s32[8]{0:T(128)}, u32[]{:S(2)}) copy-start(s32[8]{0:T(128)} %param.8) | copy-start | bytes 100
  7.2 25.6 %copy-start.11 = (s32[8]{0:T(128)S(1)}, s32[8]{0:T(128)}, u32[]{:S(2)}) copy-start(s32[8]{0:T(128)} %param.6) | copy-start | bytes 100
  7.2 2.2 %collective-permute-start.3 = (f32[128,128]{1,0:T(8,128)}, f32[128,128]{1,0:T(8,128)S(1)}, u32[]{:S(2)}, u32[]{:S(2)}) collective-permute-start(f32[128,128]{1,0:T(8,128)} %rest.1), channel_id=1, source_target_pairs={{0,1},{1,0},{2,3},{3,2},{4,5},{5,4},{6,7},{7,6},{8,9},{9,8},{10,11... | collective-permute-start | bytes 196616 | tf_op jit(solution)/shard_map/ppermute | solution.py:111
  7.3 8.1 %collective-permute-start.1 = (f32[128,128]{1,0:T(8,128)S(1)}, f32[128,128]{1,0:T(8,128)S(1)}, u32[]{:S(2)}, u32[]{:S(2)}) collective-permute-start(f32[128,128]{1,0:T(8,128)S(1)} %log_add_fusion.2), channel_id=1, source_target_pairs={{0,5},{1,6},{2,7},{3,4},{4,9},{5,10},{6,11},{7,8},{8,13},{9,14},{1... | collective-permute-start | bytes 196616 | tf_op jit(solution)/shard_map/ppermute | solution.py:111
  10.3 5.3 %collective-permute-start.4 = (f32[128,128]{1,0:T(8,128)S(1)}, f32[128,128]{1,0:T(8,128)S(1)}, u32[]{:S(2)}, u32[]{:S(2)}) collective-permute-start(f32[128,128]{1,0:T(8,128)S(1)} %log_add_fusion.1), channel_id=1, source_target_pairs={{0,2},{1,3},{2,0},{3,1},{4,6},{5,7},{6,4},{7,5},{8,10},{9,11},{10,... | collective-permute-start | bytes 196616 | tf_op jit(solution)/shard_map/ppermute | solution.py:111
  15.4 1.3 %copy-start.5 = (f32[128,128]{1,0:T(8,128)}, f32[128,128]{1,0:T(8,128)S(1)}, u32[]{:S(2)}) copy-start(f32[128,128]{1,0:T(8,128)S(1)} %collective-permute-done.1.one_ref) | copy-start | bytes 196612
  15.4 1.3 %collective-permute-start.2 = (f32[128,128]{1,0:T(8,128)S(1)}, f32[128,128]{1,0:T(8,128)S(1)}, u32[]{:S(2)}, u32[]{:S(2)}) collective-permute-start(f32[128,128]{1,0:T(8,128)S(1)} %collective-permute-done.1.one_ref), channel_id=1, source_target_pairs={{0,1},{1,0},{2,3},{3,2},{4,5},{5,4},{6,7},{7,6},{8,9},{9,8},{10,11... | collective-permute-start | bytes 196616 | tf_op jit(solution)/shard_map/ppermute | solution.py:111
  16.7 0.6 copy-start.6
  18.8 33.6 %copy-start.9 = (f32[32,128]{1,0:T(8,128)S(1)}, f32[32,128]{1,0:T(8,128)}, u32[]{:S(2)}) copy-start(f32[32,128]{1,0:T(8,128)} %get-tuple-element.8) | copy-start | bytes 49156
  18.8 1.4 %collective-permute-start.5 = (f32[2,32,128]{2,1,0:T(8,128)}, f32[2,32,128]{2,1,0:T(8,128)S(1)}, u32[]{:S(2)}, u32[]{:S(2)}) collective-permute-start(f32[2,32,128]{2,1,0:T(8,128)} %get-tuple-element.9), channel_id=1, source_target_pairs={{0,1},{1,0},{2,3},{3,2},{4,5},{5,4},{6,7},{7,6},{8,9},{9,8},{10,11... | collective-permute-start | bytes 98312 | tf_op jit(solution)/shard_map/ppermute | solution.py:111
  20.3 14.5 %collective-permute-start.6 = (f32[2,32,128]{2,1,0:T(8,128)S(1)}, f32[2,32,128]{2,1,0:T(8,128)S(1)}, u32[]{:S(2)}, u32[]{:S(2)}) collective-permute-start(f32[2,32,128]{2,1,0:T(8,128)S(1)} %pad_maximum_fusion.1), channel_id=1, source_target_pairs={{0,9},{1,10},{2,11},{3,8},{4,13},{5,14},{6,15},{7,12},{8,17},{9,18... | collective-permute-start | bytes 98312 | tf_op jit(solution)/shard_map/ppermute | solution.py:111
  20.7 14.1 %collective-permute-start.7 = (f32[2,32,128]{2,1,0:T(8,128)S(1)}, f32[2,32,128]{2,1,0:T(8,128)S(1)}, u32[]{:S(2)}, u32[]{:S(2)}) collective-permute-start(f32[2,32,128]{2,1,0:T(8,128)S(1)} %pad_maximum_fusion.2), channel_id=1, source_target_pairs={{0,13},{1,14},{2,15},{3,12},{4,9},{5,10},{6,11},{7,8},{8,21},{9,22... | collective-permute-start | bytes 98312 | tf_op jit(solution)/shard_map/ppermute | solution.py:111
  23.8 11.1 %collective-permute-start.13 = (f32[1,32,128]{2,1,0:T(8,128)S(1)}, f32[1,32,128]{2,1,0:T(8,128)S(1)}, u32[]{:S(2)}, u32[]{:S(2)}) collective-permute-start(f32[1,32,128]{2,1,0:T(8,128)S(1)} %copy-done.3), channel_id=1, source_target_pairs={{0,16},{1,17},{2,18},{3,19},{4,20},{5,21},{6,22},{7,23},{8,24},{9,... | collective-permute-start | bytes 49160 | tf_op jit(solution)/shard_map/ppermute | solution.py:111
  34.8 1.3 %copy-start.4 = (f32[2,32,128]{2,1,0:T(8,128)}, f32[2,32,128]{2,1,0:T(8,128)S(1)}, u32[]{:S(2)}) copy-start(f32[2,32,128]{2,1,0:T(8,128)S(1)} %broadcast_select_fusion.one_ref) | copy-start | bytes 98308
  34.8 1.3 %collective-permute-start.8 = (f32[2,32,128]{2,1,0:T(8,128)S(1)}, f32[2,32,128]{2,1,0:T(8,128)S(1)}, u32[]{:S(2)}, u32[]{:S(2)}) collective-permute-start(f32[2,32,128]{2,1,0:T(8,128)S(1)} %broadcast_select_fusion.one_ref), channel_id=1, source_target_pairs={{0,1},{1,0},{2,3},{3,2},{4,5},{5,4},{6,7},{7,6},{8,9},{9,8},{10,11... | collective-permute-start | bytes 98312 | tf_op jit(solution)/shard_map/ppermute | solution.py:111
  34.9 6.1 %collective-permute-start.14 = (f32[2,32,128]{2,1,0:T(8,128)S(1)}, f32[2,32,128]{2,1,0:T(8,128)S(1)}, u32[]{:S(2)}, u32[]{:S(2)}) collective-permute-start(f32[2,32,128]{2,1,0:T(8,128)S(1)} %pad_maximum_fusion.3), channel_id=1, source_target_pairs={{0,4},{1,5},{2,6},{3,7},{4,0},{5,1},{6,2},{7,3},{8,12},{9,13},{10,... | collective-permute-start | bytes 98312 | tf_op jit(solution)/shard_map/ppermute | solution.py:111
  36.1 0.6 copy-start.8
  39.0 5.7 %collective-permute-start.9 = (f32[2,32,128]{2,1,0:T(8,128)S(1)}, f32[2,32,128]{2,1,0:T(8,128)S(1)}, u32[]{:S(2)}, u32[]{:S(2)}) collective-permute-start(f32[2,32,128]{2,1,0:T(8,128)S(1)} %get-tuple-element.14), channel_id=1, source_target_pairs={{0,8},{1,9},{2,10},{3,11},{4,12},{5,13},{6,14},{7,15},{8,16},{9,17... | collective-permute-start | bytes 98312 | tf_op jit(solution)/shard_map/ppermute | solution.py:111
  40.3 6.6 %collective-permute-start.10 = (f32[2,32,128]{2,1,0:T(8,128)S(1)}, f32[2,32,128]{2,1,0:T(8,128)S(1)}, u32[]{:S(2)}, u32[]{:S(2)}) collective-permute-start(f32[2,32,128]{2,1,0:T(8,128)S(1)} %get-tuple-element.15), channel_id=1, source_target_pairs={{0,12},{1,13},{2,14},{3,15},{4,8},{5,9},{6,10},{7,11},{8,20},{9,21... | collective-permute-start | bytes 98312 | tf_op jit(solution)/shard_map/ppermute | solution.py:111
  41.0 5.9 %collective-permute-start.15 = (f32[32,128]{1,0:T(8,128)S(1)}, f32[32,128]{1,0:T(8,128)S(1)}, u32[]{:S(2)}, u32[]{:S(2)}) collective-permute-start(f32[32,128]{1,0:T(8,128)S(1)} %add_bitcast_fusion), channel_id=1, source_target_pairs={{0,8},{1,9},{2,10},{3,11},{4,12},{5,13},{6,14},{7,15},{8,0},{9,1},... | collective-permute-start | bytes 49160 | tf_op jit(solution)/shard_map/ppermute | solution.py:111
  47.0 5.5 %collective-permute-start.11 = (f32[32,128]{1,0:T(8,128)S(1)}, f32[32,128]{1,0:T(8,128)S(1)}, u32[]{:S(2)}, u32[]{:S(2)}) collective-permute-start(f32[32,128]{1,0:T(8,128)S(1)} %fusion.8), channel_id=1, source_target_pairs={{0,8},{1,9},{2,10},{3,11},{4,12},{5,13},{6,14},{7,15},{8,16},{9,17... | collective-permute-start | bytes 49160 | tf_op jit(solution)/shard_map/ppermute | solution.py:111
  53.2 4.0 %collective-permute-start.16 = (f32[2,32,128]{2,1,0:T(8,128)S(1)}, f32[2,32,128]{2,1,0:T(8,128)S(1)}, u32[]{:S(2)}, u32[]{:S(2)}) collective-permute-start(f32[2,32,128]{2,1,0:T(8,128)S(1)} %pad_maximum_fusion.4), channel_id=1, source_target_pairs={{0,2},{1,3},{2,0},{3,1},{4,6},{5,7},{6,4},{7,5},{8,10},{9,11},{10,... | collective-permute-start | bytes 98312 | tf_op jit(solution)/shard_map/ppermute | solution.py:111
  54.1 6.4 %collective-permute-start.12 = (f32[32,128]{1,0:T(8,128)S(1)}, f32[32,128]{1,0:T(8,128)S(1)}, u32[]{:S(2)}, u32[]{:S(2)}) collective-permute-start(f32[32,128]{1,0:T(8,128)S(1)} %fusion.8), channel_id=1, source_target_pairs={{0,10},{1,11},{2,8},{3,9},{4,14},{5,15},{6,12},{7,13},{8,18},{9,19... | collective-permute-start | bytes 49160 | tf_op jit(solution)/shard_map/ppermute | solution.py:111
  60.5 1.3 %copy-start.2 = (f32[4,32,128]{2,1,0:T(8,128)}, f32[4,32,128]{2,1,0:T(8,128)S(1)}, u32[]{:S(2)}) copy-start(f32[4,32,128]{2,1,0:T(8,128)S(1)} %pad_maximum_fusion.here_ref) | copy-start | bytes 196612
  60.5 1.3 %collective-permute-start.17 = (f32[4,32,128]{2,1,0:T(8,128)S(1)}, f32[4,32,128]{2,1,0:T(8,128)S(1)}, u32[]{:S(2)}, u32[]{:S(2)}) collective-permute-start(f32[4,32,128]{2,1,0:T(8,128)S(1)} %pad_maximum_fusion.here_ref), channel_id=1, source_target_pairs={{0,1},{1,0},{2,3},{3,2},{4,5},{5,4},{6,7},{7,6},{8,9},{9,8},{10,11... | collective-permute-start | bytes 196616 | tf_op jit(solution)/shard_map/ppermute | solution.py:111
  61.9 0.6 copy-start.7
